TPU v7x, 32 devices: a whole 2x2x4 slice. The times are simulated.
32 devices in a mesh: tm: 8 (over z, x), pack: 4 (over y, core).
Axes of the slice: x: 2, y: 2, z: 4, core: 2. Of those that a mesh axis runs over, the one named last changes fastest.
Arguments:
- queries: bfloat16 [4, 4096, 1024], P('pack', 'tm'), may hold values from -8 to 8
- keys: bfloat16 [4, 4096, 1024], P('pack', 'tm'), may hold values from -8 to 8
- values: bfloat16 [4, 4096, 1024], P('pack', 'tm'), may hold values from -6 to 6
- w_out: bfloat16 [1024, 1024], replicated, may hold values from -0.1875 to 0.1875
- norm_gain: float32 [1024], replicated, may hold values from 0.1 to 1.9
- block_owner: int32 [4, 32, 1], P('pack', 'tm'), may hold values from 0 to 3; in each aligned block of 4 rows (0 to 3, 4 to 7, ..., all dimensions but the last counted through in order) at most 2 rows name the same one
- block_base: int32 [4, 32], P('pack', 'tm'), may hold values from 0 to 112
- frame_offset: int32 [4, 32, 128], P('pack', 'tm'), may hold values from 0 to 15, never falling along the last dimension, each value on 1 to 16 neighbouring positions
Outputs:
- encoded: bfloat16 [4, 4096, 1024], P('pack', 'tm')
- pooled: bfloat16 [4, 1024, 1024], P('pack', 'tm')
Inputs may be any that keep to these rules, and one draw needn't show every extreme that they name: `block_owner`: among the 4 blocks of one device (aligned runs of the list), at most 2 name the same owner. `frame_offset`: within each block of 128 frames the offsets never fall and each of 0 to 15 occurs.
All inputs are finite; a program needn't handle non-finite values.
Results may differ from a plain program's by a relative error of at most 0.008.
Values may be sent and summed in bfloat16 or wider, within the bound.
No kernel may reach another device: no remote copies, remote signals or barrier semaphores. Data moves between devices by JAX's collectives and lax.ppermute only.
A program may use at most 128 MiB of HBM per device.

v0:
```python
import math
import jax
import jax.numpy as jnp
from jax import lax
from jax.sharding import PartitionSpec as P

HEADS = 16
LANDMARKS = 256
BLOCK = 128
POOL_DEV = 128


def mix_heads(query_rows, mark_keys, mark_values, head_count):
    row_count, model_width = query_rows.shape
    head_dim = model_width // head_count
    query_heads = query_rows.reshape(row_count, head_count, head_dim)
    key_heads = mark_keys.reshape(-1, head_count, head_dim)
    value_heads = mark_values.reshape(-1, head_count, head_dim)
    scores = jnp.einsum(
        "nhe,mhe->nhm", query_heads, key_heads, preferred_element_type=jnp.float32
    ) * head_dim ** (-0.5)
    weights = jnp.exp(scores - jnp.max(scores, axis=-1, keepdims=True))
    totals = jnp.sum(weights, axis=-1)
    blended = jnp.einsum(
        "nhm,mhe->nhe",
        weights.astype(jnp.bfloat16),
        value_heads,
        preferred_element_type=jnp.float32,
    )
    return (blended / totals[..., None]).reshape(row_count, model_width).astype(jnp.bfloat16)


def mix_blocked(query_rows, mark_keys, mark_values, head_count):
    row_count, model_width = query_rows.shape
    row_block = math.gcd(row_count, 1024)
    stacked = query_rows.reshape(row_count // row_block, row_block, model_width)
    mixed_rows = lax.map(
        lambda frame_block: mix_heads(frame_block, mark_keys, mark_values, head_count), stacked
    )
    return mixed_rows.reshape(row_count, model_width)


def local(queries, keys, values, w_out, norm_gain, block_owner, block_base, frame_offset):
    frame_q = queries[0]
    frame_k = keys[0]
    frame_v = values[0]
    frame_count, model_width = frame_q.shape
    span = frame_count // LANDMARKS
    mark_queries = jnp.mean(
        frame_q.reshape(LANDMARKS, span, model_width), axis=1, dtype=jnp.float32
    ).astype(jnp.bfloat16)
    mark_keys = jnp.mean(
        frame_k.reshape(LANDMARKS, span, model_width), axis=1, dtype=jnp.float32
    ).astype(jnp.bfloat16)
    mark_values = mix_heads(mark_queries, frame_k, frame_v, HEADS)
    spread_q, spread_k, spread_v = (
        lax.all_to_all(frame_q, "tm", split_axis=1, concat_axis=0, tiled=True),
        lax.all_to_all(mark_keys, "tm", split_axis=1, concat_axis=0, tiled=True),
        lax.all_to_all(mark_values, "tm", split_axis=1, concat_axis=0, tiled=True),
    )
    local_heads = HEADS // lax.axis_size("tm")
    head_result = mix_blocked(spread_q, spread_k, spread_v, local_heads)
    attended = lax.all_to_all(head_result, "tm", split_axis=0, concat_axis=1, tiled=True)
    projected = jnp.dot(attended, w_out, preferred_element_type=jnp.float32)
    scaled = projected * lax.rsqrt(jnp.mean(projected * projected, axis=-1, keepdims=True) + 1e-06)
    encoded = (scaled * norm_gain).astype(jnp.bfloat16)
    pack_count = lax.axis_size("pack")
    owners = block_owner[0, :, 0]
    block_count = owners.shape[0]
    slot_count = max(2, 2 * block_count // pack_count)
    pack_range = jnp.arange(pack_count, dtype=jnp.int32)
    dest_hits = (owners[:, None] == pack_range[None, :]).astype(jnp.int32)
    slot_rank = jnp.sum((jnp.cumsum(dest_hits, axis=0) - dest_hits) * dest_hits, axis=1)
    chosen = (owners[None, None, :] == pack_range[:, None, None]) & (
        slot_rank[None, None, :] == jnp.arange(slot_count, dtype=jnp.int32)[None, :, None]
    )
    filled = jnp.any(chosen, axis=-1)
    source_block = jnp.sum(
        chosen.astype(jnp.int32) * jnp.arange(block_count, dtype=jnp.int32)[None, None, :], axis=-1
    )
    frame_blocks = encoded.reshape(block_count, BLOCK, model_width)
    offsets = frame_offset[0]
    block_bases = block_base[0]
    sent_rows = jnp.where(
        filled[..., None, None],
        jnp.take(frame_blocks, source_block, axis=0),
        jnp.zeros((), jnp.bfloat16),
    )
    row_targets = jnp.take(block_bases, source_block)[..., None] + jnp.take(
        offsets, source_block, axis=0
    )
    sent_targets = jnp.where(filled[..., None], row_targets, -1).astype(jnp.bfloat16)
    got_rows, got_targets = (
        lax.all_to_all(sent_rows, "pack", split_axis=0, concat_axis=0, tiled=True),
        lax.all_to_all(sent_targets, "pack", split_axis=0, concat_axis=0, tiled=True),
    )
    pool_rows = jnp.arange(POOL_DEV, dtype=jnp.int32).astype(jnp.bfloat16)
    placing = got_targets[:, :, None, :] == pool_rows[None, None, :, None]
    pool_sums = jnp.einsum(
        "scrf,scfd->rd", placing.astype(jnp.bfloat16), got_rows, preferred_element_type=jnp.float32
    )
    pool_counts = jnp.sum(placing.astype(jnp.float32), axis=(0, 1, 3))
    pooled = (pool_sums / jnp.maximum(pool_counts, 1.0)[:, None]).astype(jnp.bfloat16)
    return (encoded[None], pooled[None])


def solution(mesh):
    return jax.shard_map(
        local,
        mesh=mesh,
        in_specs=(
            P("pack", "tm", None),
            P("pack", "tm", None),
            P("pack", "tm", None),
            P(),
            P(),
            P("pack", "tm", None),
            P("pack", "tm"),
            P("pack", "tm", None),
        ),
        out_specs=(P("pack", "tm", None), P("pack", "tm", None)),
        check_vma=False,
    )
```

profile of v0, /device:TPU:0, one launch (start us, length us, event | category | flops | bytes accessed | tf_op | source)
XLA Modules:
  0.0 267.6 jit_solution(12814046430353551243)
XLA Ops:
  0.7 3.6 %reshape.165 = f32[256,2,1024]{2,1,0:T(2,128)} reshape(bf16[1,512,1024]{2,1,0:T(8,128)(2,1)} %param.11) | data formatting | bytes 3145728 | tf_op jit(solution)/shard_map/convert_element_type | solution.py:52
  4.2 5.1 %reduce_sum.74 = f32[256,1024]{1,0:T(8,128)} reduce(f32[256,2,1024]{2,1,0:T(2,128)} %reshape.165, f32[]{:T(128)} %constant.55.clone.1), dimensions={1}, to_apply=%region_0.0 | reduce | flops 262144 | bytes 3145732 | tf_op jit(solution)/shard_map/reduce_sum | solution.py:52
  13.5 7.3 %all-to-all-start.1 = ((bf16[256,8,128]{0,2,1:T(8,128)(2,1)}), bf16[256,8,128]{0,2,1:T(8,128)(2,1)}, u32[]{:S(2)}, u32[]{:S(2)}) async-start(bf16[256,8,128]{0,2,1:T(8,128)(2,1)} %bitcast.126), calls=%async_computation.1 | async-start | bytes 1048576 | tf_op jit(solution)/shard_map/all_to_all | solution.py:58
  22.1 3.5 %reshape.166 = f32[256,2,1024]{2,1,0:T(2,128)} reshape(bf16[1,512,1024]{2,1,0:T(8,128)(2,1)} %param.10) | data formatting | bytes 3145728 | tf_op jit(solution)/shard_map/convert_element_type | solution.py:49
  25.6 5.1 %reduce_sum.75 = f32[256,1024]{1,0:T(8,128)} reduce(f32[256,2,1024]{2,1,0:T(2,128)} %reshape.166, f32[]{:T(128)} %constant.55.clone.1), dimensions={1}, to_apply=%region_1.0 | reduce | flops 262144 | bytes 3145732 | tf_op jit(solution)/shard_map/reduce_sum | solution.py:49
  44.8 6.1 %divide_convert_fusion = bf16[256,16,64]{0,2,1:T(8,128)(2,1)} fusion(bf16[512,16,64]{0,2,1:T(8,128)(2,1)} %bitcast.129, f32[16,256,512]{2,1,0:T(8,128)} %copy-done.3, f32[256,16]{0,1:T(8,128)S(1)} %get-tuple-element.71, f32[256,16]{0,1:T(8,128)S(1)} %fusion.16), kind=kOutput, calls=%fused_computation.30 | convolution fusion | flops 275251200 | bytes 9994240 | tf_op jit(solution)/shard_map/nhm,mhe->nhe/dot_general | solution.py:24
  51.0 6.0 %all-to-all-start.2 = ((bf16[256,8,128]{0,2,1:T(8,128)(2,1)}), bf16[256,8,128]{0,2,1:T(8,128)(2,1)}, u32[]{:S(2)}, u32[]{:S(2)}) async-start(bf16[256,8,128]{0,2,1:T(8,128)(2,1)} %bitcast.131), calls=%async_computation.2 | async-start | bytes 1048576 | tf_op jit(solution)/shard_map/all_to_all | solution.py:59
  58.3 12.7 %all-to-all-done.2 = bf16[256,8,128]{0,2,1:T(8,128)(2,1)} async-done(((bf16[256,8,128]{0,2,1:T(8,128)(2,1)}), bf16[256,8,128]{0,2,1:T(8,128)(2,1)}, u32[]{:S(2)}, u32[]{:S(2)}) %all-to-all-start.2) | async-done | bytes 524320 | tf_op jit(solution)/shard_map/all_to_all | solution.py:59
  71.0 4.2 %all-to-all-start = ((bf16[512,8,128]{0,2,1:T(8,128)(2,1)}), bf16[512,8,128]{0,2,1:T(8,128)(2,1)}, u32[]{:S(2)}, u32[]{:S(2)}) async-start(bf16[512,8,128]{0,2,1:T(8,128)(2,1)} %bitcast.124), calls=%async_computation | async-start | bytes 2097152 | tf_op jit(solution)/shard_map/all_to_all | solution.py:57
  78.8 21.8 %all-to-all-done = bf16[512,8,128]{0,2,1:T(8,128)(2,1)} async-done(((bf16[512,8,128]{0,2,1:T(8,128)(2,1)}), bf16[512,8,128]{0,2,1:T(8,128)(2,1)}, u32[]{:S(2)}, u32[]{:S(2)}) %all-to-all-start) | async-done | bytes 1048608 | tf_op jit(solution)/shard_map/all_to_all | solution.py:57
  102.8 89.4 %while.10 = (s32[]{:T(128)}, bf16[4,1024,128]{2,1,0:T(8,128)(2,1)}, bf16[4,1024,128]{2,1,0:T(8,128)(2,1)}, bf16[2048,128]{0,1:T(8,128)(2,1)S(1)}, bf16[2048,128]{0,1:T(8,128)(2,1)}, /*index=5*/s32[]{:T(128)}) while((s32[]{:T(128)}, bf16[4,1024,128]{2,1,0:T(8,128)(2,1)}, bf16[4,1024,128]{2,1,0:T(8,128)(2,1)}, bf16[2048,128]{0,1:T(8,128)(2,1)S(1)}, ...), condition=%wide.region_7.8_spmd, body=%wide.region_4.7_spmd.sunk | while | flops 1107554304 | bytes 121151608 | solution.py:37
  106.5 5.7 %copy-done.2 = f32[2,1024,2048]{2,1,0:T(8,128)} copy-done((f32[2,1024,2048]{2,1,0:T(8,128)}, f32[2,1024,2048]{2,1,0:T(8,128)S(1)}, u32[]{:S(2)}) %copy-start.2) | copy-done | bytes 16777240 | tf_op jit(solution)/shard_map/while
  115.4 8.9 %fusion.68 = bf16[1024,2,64]{0,2,1:T(8,128)(2,1)S(1)} fusion(bf16[2048,2,64]{0,2,1:T(8,128)(2,1)} %bitcast.110, f32[2,1024,2048]{2,1,0:T(8,128)} %copy-done.2, f32[1024,2]{0,1:T(2,128)S(1)} %get-tuple-element.109, f32[1024,2]{0,1:T(2,128)S(1)} %fusion.67), kind=kOutput, calls=%fused_computation.11.clone.1 | convolution fusion | flops 549715968 | bytes 17580032 | tf_op jit(solution)/shard_map/while/body/eval_jaxpr/nhm,mhe->nhe/dot_general | solution.py:24
  128.8 5.7 %copy-done.2 = f32[2,1024,2048]{2,1,0:T(8,128)} copy-done((f32[2,1024,2048]{2,1,0:T(8,128)}, f32[2,1024,2048]{2,1,0:T(8,128)S(1)}, u32[]{:S(2)}) %copy-start.2) | copy-done | bytes 16777240 | tf_op jit(solution)/shard_map/while
  134.5 3.3 %fusion.67 = f32[1024,2]{0,1:T(2,128)S(1)} fusion(f32[2,1024,2048]{2,1,0:T(8,128)S(1)} %get-tuple-element.108, f32[1024,2]{0,1:T(2,128)S(1)} %get-tuple-element.109), kind=kLoop, calls=%fused_computation.6.clone.1 | loop fusion | flops 12580864 | bytes 16793600 | tf_op jit(solution)/shard_map/while/body/eval_jaxpr/reduce_sum | solution.py:23
  137.8 8.8 %fusion.68 = bf16[1024,2,64]{0,2,1:T(8,128)(2,1)S(1)} fusion(bf16[2048,2,64]{0,2,1:T(8,128)(2,1)} %bitcast.110, f32[2,1024,2048]{2,1,0:T(8,128)} %copy-done.2, f32[1024,2]{0,1:T(2,128)S(1)} %get-tuple-element.109, f32[1024,2]{0,1:T(2,128)S(1)} %fusion.67), kind=kOutput, calls=%fused_computation.11.clone.1 | convolution fusion | flops 549715968 | bytes 17580032 | tf_op jit(solution)/shard_map/while/body/eval_jaxpr/nhm,mhe->nhe/dot_general | solution.py:24
  151.1 5.7 %copy-done.2 = f32[2,1024,2048]{2,1,0:T(8,128)} copy-done((f32[2,1024,2048]{2,1,0:T(8,128)}, f32[2,1024,2048]{2,1,0:T(8,128)S(1)}, u32[]{:S(2)}) %copy-start.2) | copy-done | bytes 16777240 | tf_op jit(solution)/shard_map/while
  160.1 8.8 %fusion.68 = bf16[1024,2,64]{0,2,1:T(8,128)(2,1)S(1)} fusion(bf16[2048,2,64]{0,2,1:T(8,128)(2,1)} %bitcast.110, f32[2,1024,2048]{2,1,0:T(8,128)} %copy-done.2, f32[1024,2]{0,1:T(2,128)S(1)} %get-tuple-element.109, f32[1024,2]{0,1:T(2,128)S(1)} %fusion.67), kind=kOutput, calls=%fused_computation.11.clone.1 | convolution fusion | flops 549715968 | bytes 17580032 | tf_op jit(solution)/shard_map/while/body/eval_jaxpr/nhm,mhe->nhe/dot_general | solution.py:24
  173.5 5.7 %copy-done.2 = f32[2,1024,2048]{2,1,0:T(8,128)} copy-done((f32[2,1024,2048]{2,1,0:T(8,128)}, f32[2,1024,2048]{2,1,0:T(8,128)S(1)}, u32[]{:S(2)}) %copy-start.2) | copy-done | bytes 16777240 | tf_op jit(solution)/shard_map/while
  182.4 8.8 %fusion.68 = bf16[1024,2,64]{0,2,1:T(8,128)(2,1)S(1)} fusion(bf16[2048,2,64]{0,2,1:T(8,128)(2,1)} %bitcast.110, f32[2,1024,2048]{2,1,0:T(8,128)} %copy-done.2, f32[1024,2]{0,1:T(2,128)S(1)} %get-tuple-element.109, f32[1024,2]{0,1:T(2,128)S(1)} %fusion.67), kind=kOutput, calls=%fused_computation.11.clone.1 | convolution fusion | flops 549715968 | bytes 17580032 | tf_op jit(solution)/shard_map/while/body/eval_jaxpr/nhm,mhe->nhe/dot_general | solution.py:24
  192.2 3.7 %all-to-all-start.3 = ((bf16[8,512,128]{2,1,0:T(8,128)(2,1)}), bf16[8,512,128]{2,1,0:T(8,128)(2,1)S(1)}, u32[]{:S(2)}, u32[]{:S(2)}) async-start(bf16[8,512,128]{2,1,0:T(8,128)(2,1)} %bitcast.128), calls=%async_computation.3 | async-start | bytes 2097152 | tf_op jit(solution)/shard_map/all_to_all | solution.py:63
  199.1 22.5 %all-to-all-done.3 = bf16[8,512,128]{2,1,0:T(8,128)(2,1)S(1)} async-done(((bf16[8,512,128]{2,1,0:T(8,128)(2,1)}), bf16[8,512,128]{2,1,0:T(8,128)(2,1)S(1)}, u32[]{:S(2)}, u32[]{:S(2)}) %all-to-all-start.3) | async-done | bytes 1048608 | tf_op jit(solution)/shard_map/all_to_all | solution.py:63
  234.6 4.4 %all-to-all-start.5 = ((bf16[4,2,128,1024]{3,2,1,0:T(8,128)(2,1)}), bf16[4,2,128,1024]{3,2,1,0:T(8,128)(2,1)}, u32[]{:S(2)}, u32[]{:S(2)}) async-start(bf16[4,2,128,1024]{3,2,1,0:T(8,128)(2,1)} %select_select_fusion), calls=%async_computation.5 | async-start | bytes 4194304 | tf_op jit(solution)/shard_map/all_to_all | solution.py:94
  242.1 22.7 %all-to-all-done.5 = bf16[4,2,128,1024]{3,2,1,0:T(8,128)(2,1)} async-done(((bf16[4,2,128,1024]{3,2,1,0:T(8,128)(2,1)}), bf16[4,2,128,1024]{3,2,1,0:T(8,128)(2,1)}, u32[]{:S(2)}, u32[]{:S(2)}) %all-to-all-start.5) | async-done | bytes 2097184 | tf_op jit(solution)/shard_map/all_to_all | solution.py:94
  (97 shorter events, 76.5 us)
Async XLA Ops:
  0.6 225.8 %copy-start = (bf16[1024,1024]{1,0:T(8,128)(2,1)S(1)}, bf16[1024,1024]{1,0:T(8,128)(2,1)}, u32[]{:S(2)}) copy-start(bf16[1024,1024]{1,0:T(8,128)(2,1)} %param.13) | copy-start | bytes 6291460
  0.6 20.1 %copy-start.5 = (bf16[1,512,1024]{2,1,0:T(8,128)(2,1)S(1)}, bf16[1,512,1024]{2,1,0:T(8,128)(2,1)}, u32[]{:S(2)}) copy-start(bf16[1,512,1024]{2,1,0:T(8,128)(2,1)} %param.11) | copy-start | bytes 3145732
  13.5 37.5 %all-to-all-start.1 = ((bf16[256,8,128]{0,2,1:T(8,128)(2,1)}), bf16[256,8,128]{0,2,1:T(8,128)(2,1)}, u32[]{:S(2)}, u32[]{:S(2)}) async-start(bf16[256,8,128]{0,2,1:T(8,128)(2,1)} %bitcast.126), calls=%async_computation.1 | async-start | bytes 1048576 | tf_op jit(solution)/shard_map/all_to_all | solution.py:58
  22.1 12.7 %copy-start.7 = (bf16[1,512,1024]{1,2,0:T(8,128)(2,1)S(1)}, bf16[1,512,1024]{1,2,0:T(8,128)(2,1)}, u32[]{:S(2)}) copy-start(bf16[1,512,1024]{1,2,0:T(8,128)(2,1)} %copy.83) | copy-start | bytes 3145732
  37.2 3.2 %copy-start.3 = (f32[16,256,512]{2,1,0:T(8,128)}, f32[16,256,512]{2,1,0:T(8,128)S(1)}, u32[]{:S(2)}) copy-start(f32[16,256,512]{2,1,0:T(8,128)S(1)} %get-tuple-element.72) | copy-start | bytes 25165828
  42.5 14.5 %copy-start.6 = (bf16[1,512,1024]{2,1,0:T(8,128)(2,1)S(1)}, bf16[1,512,1024]{2,1,0:T(8,128)(2,1)}, u32[]{:S(2)}) copy-start(bf16[1,512,1024]{2,1,0:T(8,128)(2,1)} %param.10) | copy-start | bytes 3145732
  51.0 20.1 %all-to-all-start.2 = ((bf16[256,8,128]{0,2,1:T(8,128)(2,1)}), bf16[256,8,128]{0,2,1:T(8,128)(2,1)}, u32[]{:S(2)}, u32[]{:S(2)}) async-start(bf16[256,8,128]{0,2,1:T(8,128)(2,1)} %bitcast.131), calls=%async_computation.2 | async-start | bytes 1048576 | tf_op jit(solution)/shard_map/all_to_all | solution.py:59
  71.0 29.5 %all-to-all-start = ((bf16[512,8,128]{0,2,1:T(8,128)(2,1)}), bf16[512,8,128]{0,2,1:T(8,128)(2,1)}, u32[]{:S(2)}, u32[]{:S(2)}) async-start(bf16[512,8,128]{0,2,1:T(8,128)(2,1)} %bitcast.124), calls=%async_computation | async-start | bytes 2097152 | tf_op jit(solution)/shard_map/all_to_all | solution.py:57
  102.8 93.1 %copy-start.11 = (s32[1,4,1]{1,2,0:T(1,128)S(1)}, s32[1,4,1]{1,2,0:T(1,128)}, u32[]{:S(2)}) copy-start(s32[1,4,1]{1,2,0:T(1,128)} %param.15) | copy-start | bytes 52
  102.8 93.8 %copy-start.1 = (s32[1,4]{1,0:T(1,128)S(1)}, s32[1,4]{1,0:T(1,128)}, u32[]{:S(2)}) copy-start(s32[1,4]{1,0:T(1,128)} %param.16) | copy-start | bytes 52
  102.8 95.0 %copy-start.9 = (s32[1,4,128]{2,1,0:T(4,128)S(1)}, s32[1,4,128]{2,1,0:T(4,128)}, u32[]{:S(2)}) copy-start(s32[1,4,128]{2,1,0:T(4,128)} %param.17) | copy-start | bytes 6148
  106.5 5.7 %copy-start.2 = (f32[2,1024,2048]{2,1,0:T(8,128)}, f32[2,1024,2048]{2,1,0:T(8,128)S(1)}, u32[]{:S(2)}) copy-start(f32[2,1024,2048]{2,1,0:T(8,128)S(1)} %get-tuple-element.108) | copy-start | bytes 50331652 | tf_op jit(solution)/shard_map/while
  128.8 5.7 %copy-start.2 = (f32[2,1024,2048]{2,1,0:T(8,128)}, f32[2,1024,2048]{2,1,0:T(8,128)S(1)}, u32[]{:S(2)}) copy-start(f32[2,1024,2048]{2,1,0:T(8,128)S(1)} %get-tuple-element.108) | copy-start | bytes 50331652 | tf_op jit(solution)/shard_map/while
  151.1 5.7 %copy-start.2 = (f32[2,1024,2048]{2,1,0:T(8,128)}, f32[2,1024,2048]{2,1,0:T(8,128)S(1)}, u32[]{:S(2)}) copy-start(f32[2,1024,2048]{2,1,0:T(8,128)S(1)} %get-tuple-element.108) | copy-start | bytes 50331652 | tf_op jit(solution)/shard_map/while
  173.5 5.7 %copy-start.2 = (f32[2,1024,2048]{2,1,0:T(8,128)}, f32[2,1024,2048]{2,1,0:T(8,128)S(1)}, u32[]{:S(2)}) copy-start(f32[2,1024,2048]{2,1,0:T(8,128)S(1)} %get-tuple-element.108) | copy-start | bytes 50331652 | tf_op jit(solution)/shard_map/while
  192.2 36.9 %copy-start.10 = (f32[1024]{0:T(1024)S(1)}, f32[1024]{0:T(1024)}, u32[]{:S(2)}) copy-start(f32[1024]{0:T(1024)} %param.14) | copy-start | bytes 12292
  192.2 29.5 %all-to-all-start.3 = ((bf16[8,512,128]{2,1,0:T(8,128)(2,1)}), bf16[8,512,128]{2,1,0:T(8,128)(2,1)S(1)}, u32[]{:S(2)}, u32[]{:S(2)}) async-start(bf16[8,512,128]{2,1,0:T(8,128)(2,1)} %bitcast.128), calls=%async_computation.3 | async-start | bytes 2097152 | tf_op jit(solution)/shard_map/all_to_all | solution.py:63
  221.7 3.2 %copy-start.8 = (bf16[8,512,128]{2,1,0:T(8,128)(2,1)}, bf16[8,512,128]{2,1,0:T(8,128)(2,1)S(1)}, u32[]{:S(2)}) copy-start(bf16[8,512,128]{2,1,0:T(8,128)(2,1)S(1)} %all-to-all-done.3) | copy-start | bytes 3145732
  221.7 12.9 %all-to-all-start.4 = ((bf16[4,2,128]{2,1,0:T(2,128)(2,1)}), bf16[4,2,128]{2,1,0:T(2,128)(2,1)S(1)}, u32[]{:S(2)}, u32[]{:S(2)}) async-start(bf16[4,2,128]{2,1,0:T(2,128)(2,1)} %select_convert_fusion), calls=%async_computation.4 | async-start | bytes 4096 | tf_op jit(solution)/shard_map/all_to_all | solution.py:95
  227.8 1.4 copy-start.4
  234.6 30.2 %all-to-all-start.5 = ((bf16[4,2,128,1024]{3,2,1,0:T(8,128)(2,1)}), bf16[4,2,128,1024]{3,2,1,0:T(8,128)(2,1)}, u32[]{:S(2)}, u32[]{:S(2)}) async-start(bf16[4,2,128,1024]{3,2,1,0:T(8,128)(2,1)} %select_select_fusion), calls=%async_computation.5 | async-start | bytes 4194304 | tf_op jit(solution)/shard_map/all_to_all | solution.py:94
where the time goes:
time: 269 us; the launch traced here: 268 us
  waiting for transfers between devices  79.7 us (30%)
  local copies, waits for them, and re-layouts  62.9 us (23%)
  matrix products  58 us (22%)
  other arithmetic  37.1 us (14%)
  starting transfers between devices  28.9 us (11%)
    dot_general x5, matrix products, mix_heads(): jnp.einsum('nhm,mhe->nhe', weights.astype(jnp.bfloat16), value_heads, pre...  41.5 us
    while x8, local copies, waits for them, and re-layouts  22.9 us
    all_to_all x1, waiting for transfers between devices, local(): lax.all_to_all(sent_rows, 'pack', split_axis=0, concat_axis=0, tiled=True)  22.7 us
    all_to_all x1, waiting for transfers between devices, local(): lax.all_to_all(head_result, 'tm', split_axis=0, concat_axis=1, tiled=True)  22.5 us
    all_to_all x1, waiting for transfers between devices, local(): lax.all_to_all(frame_q, 'tm', split_axis=1, concat_axis=0, tiled=True)  21.8 us
    reduce_sum x5, other arithmetic, mix_heads(): totals = jnp.sum(weights, axis=-1)  15 us
    all_to_all x1, waiting for transfers between devices, local(): lax.all_to_all(mark_values, 'tm', split_axis=1, concat_axis=0, tiled=True)  12.7 us
    dot_general x5, matrix products, mix_heads(): jnp.einsum('nhe,mhe->nhm', query_heads, key_heads, preferred_element_type...  12.3 us
  transfers between devices with their start and end apart: 6, of which 4 were waited for; matrix products, arithmetic and copies ran while one was open for 17% of the time, Pallas kernels for 0%

commit v1 on v0

--- a/solution.py
+++ b/solution.py
@@ -8,6 +8,30 @@
 LANDMARKS = 256
 BLOCK = 128
 POOL_DEV = 128
+
+
+def do_the_roads(x0, d0, block_here):
+    view_out, p_next = (x0.shape[:d0], x0.shape[d0 + 1 :])
+    return jnp.moveaxis(x0.reshape(*view_out, block_here, -1, *p_next), d0, 0)
+
+
+def handle_lane_here(slab_in, which_dim):
+    v1 = list(slab_in.shape[1:])
+    v1[which_dim] *= slab_in.shape[0]
+    return jnp.moveaxis(slab_in, 0, which_dim).reshape(v1)
+
+
+def convert_view(state, mesh_ax, obj, s0):
+    oldest, last = (lax.psum(1, mesh_ax), lax.axis_index(mesh_ax))
+    inter = do_the_roads(state, obj, oldest)
+    fields = [inter[last]]
+    m = 1
+    while m < oldest:
+        even = inter[last ^ m]
+        fields.append(lax.ppermute(even, mesh_ax, [(ix, ix ^ m) for ix in range(oldest)]))
+        m = m + 1
+    inter = jnp.stack(fields, 0)[last ^ jnp.arange(oldest)]
+    return handle_lane_here(inter, s0)
 
 
 def mix_heads(query_rows, mark_keys, mark_values, head_count):
@@ -56,7 +80,7 @@
     spread_q, spread_k, spread_v = (
         lax.all_to_all(frame_q, "tm", split_axis=1, concat_axis=0, tiled=True),
         lax.all_to_all(mark_keys, "tm", split_axis=1, concat_axis=0, tiled=True),
-        lax.all_to_all(mark_values, "tm", split_axis=1, concat_axis=0, tiled=True),
+        convert_view(mark_values, "tm", 1, 0),
     )
     local_heads = HEADS // lax.axis_size("tm")
     head_result = mix_blocked(spread_q, spread_k, spread_v, local_heads)

time: 269 us -> 257 us (0.955)
  waiting for transfers between devices: 79.7 us -> 60.4 us
  starting transfers between devices: 28.9 us -> 40.8 us
  local copies, waits for them, and re-layouts: 62.9 us -> 58.5 us
    all_to_all x1, waiting for transfers between devices: 21.8 us -> 1.64 us  [local(): lax.all_to_all(frame_q, 'tm', split_axis=1, concat_axis=0, tiled=True)]
    ppermute x0 -> x7, waiting for transfers between devices: none -> 13.7 us  [convert_view(): lax.ppermute(even, mesh_ax, [(ix, ix ^ m) for ix in range(oldest)])]
    ppermute x0 -> x7, starting transfers between devices: none -> 13.4 us  [convert_view(): lax.ppermute(even, mesh_ax, [(ix, ix ^ m) for ix in range(oldest)])]
    while x8, local copies, waits for them, and re-layouts: 22.9 us -> 9.79 us
    all_to_all x1 -> x0, waiting for transfers between devices: 12.7 us -> none  [local(): lax.all_to_all(mark_values, 'tm', split_axis=1, concat_axis=0, tiled=True)]
    another operation x0 -> x11, local copies, waits for them, and re-layouts: none -> 6.2 us
    all_to_all x1 -> x0, starting transfers between devices: 5.99 us -> none  [local(): lax.all_to_all(mark_values, 'tm', split_axis=1, concat_axis=0, tiled=True)]
    all_to_all x1, starting transfers between devices: 3.69 us -> 7.89 us  [local(): lax.all_to_all(head_result, 'tm', split_axis=0, concat_axis=1, tiled=True)]
  transfers between devices with their start and end apart: 6 -> 12, of which waited for: 4 -> 5; matrix products, arithmetic and copies ran while one was open for 17% -> 21% of each run, Pallas kernels for 0% -> 0%
where the time goes in v1:
time: 257 us; the launch traced here: 255 us
  waiting for transfers between devices  60.4 us (24%)
  local copies, waits for them, and re-layouts  58.5 us (23%)
  matrix products  57.2 us (22%)
  starting transfers between devices  40.8 us (16%)
  other arithmetic  37.1 us (14%)
    dot_general x5, matrix products, mix_heads(): jnp.einsum('nhm,mhe->nhe', weights.astype(jnp.bfloat16), value_heads, pre...  40.7 us
    all_to_all x1, waiting for transfers between devices, local(): lax.all_to_all(sent_rows, 'pack', split_axis=0, concat_axis=0, tiled=True)  22.7 us
    all_to_all x1, waiting for transfers between devices, local(): lax.all_to_all(head_result, 'tm', split_axis=0, concat_axis=1, tiled=True)  22.4 us
    reduce_sum x5, other arithmetic, mix_heads(): totals = jnp.sum(weights, axis=-1)  15.1 us
    ppermute x7, waiting for transfers between devices, convert_view(): lax.ppermute(even, mesh_ax, [(ix, ix ^ m) for ix in range(oldest)])  13.7 us
    ppermute x7, starting transfers between devices, convert_view(): lax.ppermute(even, mesh_ax, [(ix, ix ^ m) for ix in range(oldest)])  13.4 us
    unnamed x34, local copies, waits for them, and re-layouts  13.1 us
    dot_general x5, matrix products, mix_heads(): jnp.einsum('nhe,mhe->nhm', query_heads, key_heads, preferred_element_type...  12.3 us
  transfers between devices with their start and end apart: 12, of which 5 were waited for; matrix products, arithmetic and copies ran while one was open for 21% of the time, Pallas kernels for 0%

profile of v1, /device:TPU:0, one launch (start us, length us, event | category | flops | bytes accessed | tf_op | source)
XLA Modules:
  0.0 255.2 jit_solution(1806014621857053513)
XLA Ops:
  0.7 3.6 %reshape.191 = f32[256,2,1024]{2,1,0:T(2,128)} reshape(bf16[1,512,1024]{2,1,0:T(8,128)(2,1)} %param.11) | data formatting | bytes 3145728 | tf_op jit(solution)/shard_map/convert_element_type | solution.py:76
  4.2 5.1 %reduce_sum.74 = f32[256,1024]{1,0:T(8,128)} reduce(f32[256,2,1024]{2,1,0:T(2,128)} %reshape.191, f32[]{:T(128)} %constant.45.clone.1), dimensions={1}, to_apply=%region_0.0 | reduce | flops 262144 | bytes 3145732 | tf_op jit(solution)/shard_map/reduce_sum | solution.py:76
  13.4 7.3 %all-to-all-start.1 = ((bf16[256,8,128]{0,2,1:T(8,128)(2,1)}), bf16[256,8,128]{0,2,1:T(8,128)(2,1)}, u32[]{:S(2)}, u32[]{:S(2)}) async-start(bf16[256,8,128]{0,2,1:T(8,128)(2,1)} %bitcast.157), calls=%async_computation.1 | async-start | bytes 1048576 | tf_op jit(solution)/shard_map/all_to_all | solution.py:82
  22.1 3.5 %reshape.192 = f32[256,2,1024]{2,1,0:T(2,128)} reshape(bf16[1,512,1024]{2,1,0:T(8,128)(2,1)} %param.10) | data formatting | bytes 3145728 | tf_op jit(solution)/shard_map/convert_element_type | solution.py:73
  25.5 5.1 %reduce_sum.75 = f32[256,1024]{1,0:T(8,128)} reduce(f32[256,2,1024]{2,1,0:T(2,128)} %reshape.192, f32[]{:T(128)} %constant.45.clone.1), dimensions={1}, to_apply=%region_1.0 | reduce | flops 262144 | bytes 3145732 | tf_op jit(solution)/shard_map/reduce_sum | solution.py:73
  37.2 3.2 %copy-done.3 = f32[16,256,512]{2,1,0:T(8,128)} copy-done((f32[16,256,512]{2,1,0:T(8,128)}, f32[16,256,512]{2,1,0:T(8,128)S(1)}, u32[]{:S(2)}) %copy-start.3) | copy-done | bytes 8388632
  44.8 5.3 %divide_convert_fusion = bf16[256,16,64]{0,2,1:T(8,128)(2,1)S(1)} fusion(bf16[512,16,64]{0,2,1:T(8,128)(2,1)} %bitcast.160, f32[16,256,512]{2,1,0:T(8,128)} %copy-done.3, f32[256,16]{0,1:T(8,128)S(1)} %get-tuple-element.79, f32[256,16]{0,1:T(8,128)S(1)} %fusion.16), kind=kOutput, calls=%fused_computation.31 | convolution fusion | flops 275251200 | bytes 9994240 | tf_op jit(solution)/shard_map/nhm,mhe->nhe/dot_general | solution.py:48
  64.4 4.6 %all-to-all-start = ((bf16[512,8,128]{0,2,1:T(8,128)(2,1)}), bf16[512,8,128]{0,2,1:T(8,128)(2,1)}, u32[]{:S(2)}, u32[]{:S(2)}) async-start(bf16[512,8,128]{0,2,1:T(8,128)(2,1)} %bitcast.154), calls=%async_computation | async-start | bytes 2097152 | tf_op jit(solution)/shard_map/all_to_all | solution.py:81
  69.2 3.9 %collective-permute-start.5 = (bf16[256,128]{1,0:T(8,128)(2,1)S(1)}, bf16[256,128]{1,0:T(8,128)(2,1)S(1)}, u32[]{:S(2)}, u32[]{:S(2)}) collective-permute-start(bf16[256,128]{1,0:T(8,128)(2,1)S(1)} %bitcast.169), channel_id=1, source_target_pairs={{0,24},{4,28},{8,16},{12,20},{16,8},{20,12},{24,0},{28,4},{1,25},{... | collective-permute-start | bytes 196616 | tf_op jit(solution)/shard_map/ppermute | solution.py:31
  78.1 12.1 %collective-permute-done.5 = bf16[256,128]{1,0:T(8,128)(2,1)S(1)} collective-permute-done((bf16[256,128]{1,0:T(8,128)(2,1)S(1)}, bf16[256,128]{1,0:T(8,128)(2,1)S(1)}, u32[]{:S(2)}, u32[]{:S(2)}) %collective-permute-start.5) | collective-permute-done | bytes 65568 | tf_op jit(solution)/shard_map/ppermute | solution.py:31
  99.4 76.4 %while.11 = (s32[]{:T(128)}, bf16[4,1024,128]{2,1,0:T(8,128)(2,1)}, bf16[4,1024,128]{2,1,0:T(8,128)(2,1)}, bf16[2048,128]{0,1:T(8,128)(2,1)S(1)}, bf16[8,256,128...) while((s32[]{:T(128)}, bf16[4,1024,128]{2,1,0:T(8,128)(2,1)}, ...), condition=%wide.wide.region_7.8_spmd, body=%wide.wide.region_4.7_spmd.sunk | while | flops 1107554304 | bytes 121152104 | solution.py:61
  103.1 3.3 %fusion.74 = f32[1024,2]{0,1:T(2,128)S(1)} fusion(f32[2,1024,2048]{2,1,0:T(8,128)S(1)} %get-tuple-element.144, f32[1024,2]{0,1:T(2,128)S(1)} %get-tuple-element.145), kind=kLoop, calls=%fused_computation.7.clone.clone.1 | loop fusion | flops 12580864 | bytes 16793600 | tf_op jit(solution)/shard_map/while/body/eval_jaxpr/reduce_sum | solution.py:47
  108.8 8.8 %fusion.75 = bf16[1024,2,64]{0,2,1:T(8,128)(2,1)S(1)} fusion(bf16[2048,2,64]{0,2,1:T(8,128)(2,1)} %get-tuple-element.165, f32[2,1024,2048]{2,1,0:T(8,128)} %copy-done.2, f32[1024,2]{0,1:T(2,128)S(1)} %get-tuple-element.145, f32[1024,2]{0,1:T(2,128)S(1)} %fusion.74), kind=kOutput, calls=%fused_computation.12.clone.clone.1 | convolution fusion | flops 549715968 | bytes 17580032 | tf_op jit(solution)/shard_map/while/body/eval_jaxpr/nhm,mhe->nhe/dot_general | solution.py:48
  122.2 3.3 %fusion.74 = f32[1024,2]{0,1:T(2,128)S(1)} fusion(f32[2,1024,2048]{2,1,0:T(8,128)S(1)} %get-tuple-element.144, f32[1024,2]{0,1:T(2,128)S(1)} %get-tuple-element.145), kind=kLoop, calls=%fused_computation.7.clone.clone.1 | loop fusion | flops 12580864 | bytes 16793600 | tf_op jit(solution)/shard_map/while/body/eval_jaxpr/reduce_sum | solution.py:47
  127.9 8.8 %fusion.75 = bf16[1024,2,64]{0,2,1:T(8,128)(2,1)S(1)} fusion(bf16[2048,2,64]{0,2,1:T(8,128)(2,1)} %get-tuple-element.165, f32[2,1024,2048]{2,1,0:T(8,128)} %copy-done.2, f32[1024,2]{0,1:T(2,128)S(1)} %get-tuple-element.145, f32[1024,2]{0,1:T(2,128)S(1)} %fusion.74), kind=kOutput, calls=%fused_computation.12.clone.clone.1 | convolution fusion | flops 549715968 | bytes 17580032 | tf_op jit(solution)/shard_map/while/body/eval_jaxpr/nhm,mhe->nhe/dot_general | solution.py:48
  141.3 3.3 %fusion.74 = f32[1024,2]{0,1:T(2,128)S(1)} fusion(f32[2,1024,2048]{2,1,0:T(8,128)S(1)} %get-tuple-element.144, f32[1024,2]{0,1:T(2,128)S(1)} %get-tuple-element.145), kind=kLoop, calls=%fused_computation.7.clone.clone.1 | loop fusion | flops 12580864 | bytes 16793600 | tf_op jit(solution)/shard_map/while/body/eval_jaxpr/reduce_sum | solution.py:47
  147.0 8.8 %fusion.75 = bf16[1024,2,64]{0,2,1:T(8,128)(2,1)S(1)} fusion(bf16[2048,2,64]{0,2,1:T(8,128)(2,1)} %get-tuple-element.165, f32[2,1024,2048]{2,1,0:T(8,128)} %copy-done.2, f32[1024,2]{0,1:T(2,128)S(1)} %get-tuple-element.145, f32[1024,2]{0,1:T(2,128)S(1)} %fusion.74), kind=kOutput, calls=%fused_computation.12.clone.clone.1 | convolution fusion | flops 549715968 | bytes 17580032 | tf_op jit(solution)/shard_map/while/body/eval_jaxpr/nhm,mhe->nhe/dot_general | solution.py:48
  160.4 3.3 %fusion.74 = f32[1024,2]{0,1:T(2,128)S(1)} fusion(f32[2,1024,2048]{2,1,0:T(8,128)S(1)} %get-tuple-element.144, f32[1024,2]{0,1:T(2,128)S(1)} %get-tuple-element.145), kind=kLoop, calls=%fused_computation.7.clone.clone.1 | loop fusion | flops 12580864 | bytes 16793600 | tf_op jit(solution)/shard_map/while/body/eval_jaxpr/reduce_sum | solution.py:47
  166.1 8.8 %fusion.75 = bf16[1024,2,64]{0,2,1:T(8,128)(2,1)S(1)} fusion(bf16[2048,2,64]{0,2,1:T(8,128)(2,1)} %get-tuple-element.165, f32[2,1024,2048]{2,1,0:T(8,128)} %copy-done.2, f32[1024,2]{0,1:T(2,128)S(1)} %get-tuple-element.145, f32[1024,2]{0,1:T(2,128)S(1)} %fusion.74), kind=kOutput, calls=%fused_computation.12.clone.clone.1 | convolution fusion | flops 549715968 | bytes 17580032 | tf_op jit(solution)/shard_map/while/body/eval_jaxpr/nhm,mhe->nhe/dot_general | solution.py:48
  175.8 7.9 %all-to-all-start.2 = ((bf16[8,512,128]{2,1,0:T(8,128)(2,1)}), bf16[8,512,128]{2,1,0:T(8,128)(2,1)S(1)}, u32[]{:S(2)}, u32[]{:S(2)}) async-start(bf16[8,512,128]{2,1,0:T(8,128)(2,1)} %bitcast.159), calls=%async_computation.2 | async-start | bytes 2097152 | tf_op jit(solution)/shard_map/all_to_all | solution.py:87
  186.9 22.4 %all-to-all-done.2 = bf16[8,512,128]{2,1,0:T(8,128)(2,1)S(1)} async-done(((bf16[8,512,128]{2,1,0:T(8,128)(2,1)}), bf16[8,512,128]{2,1,0:T(8,128)(2,1)S(1)}, u32[]{:S(2)}, u32[]{:S(2)}) %all-to-all-start.2) | async-done | bytes 1048608 | tf_op jit(solution)/shard_map/all_to_all | solution.py:87
  209.3 3.2 %all-to-all-start.3 = ((bf16[4,2,128]{2,1,0:T(2,128)(2,1)}), bf16[4,2,128]{2,1,0:T(2,128)(2,1)S(1)}, u32[]{:S(2)}, u32[]{:S(2)}) async-start(bf16[4,2,128]{2,1,0:T(2,128)(2,1)} %select_convert_fusion), calls=%async_computation.3 | async-start | bytes 4096 | tf_op jit(solution)/shard_map/all_to_all | solution.py:119
  222.2 4.4 %all-to-all-start.4 = ((bf16[4,2,128,1024]{3,2,1,0:T(8,128)(2,1)}), bf16[4,2,128,1024]{3,2,1,0:T(8,128)(2,1)}, u32[]{:S(2)}, u32[]{:S(2)}) async-start(bf16[4,2,128,1024]{3,2,1,0:T(8,128)(2,1)} %select_select_fusion), calls=%async_computation.4 | async-start | bytes 4194304 | tf_op jit(solution)/shard_map/all_to_all | solution.py:118
  229.7 22.7 %all-to-all-done.4 = bf16[4,2,128,1024]{3,2,1,0:T(8,128)(2,1)} async-done(((bf16[4,2,128,1024]{3,2,1,0:T(8,128)(2,1)}), bf16[4,2,128,1024]{3,2,1,0:T(8,128)(2,1)}, u32[]{:S(2)}, u32[]{:S(2)}) %all-to-all-start.4) | async-done | bytes 2097184 | tf_op jit(solution)/shard_map/all_to_all | solution.py:118
  (132 shorter events, 91.5 us)
Async XLA Ops:
  0.6 213.4 %copy-start = (bf16[1024,1024]{1,0:T(8,128)(2,1)S(1)}, bf16[1024,1024]{1,0:T(8,128)(2,1)}, u32[]{:S(2)}) copy-start(bf16[1024,1024]{1,0:T(8,128)(2,1)} %param.13) | copy-start | bytes 6291460
  0.6 20.1 %copy-start.5 = (bf16[1,512,1024]{2,1,0:T(8,128)(2,1)S(1)}, bf16[1,512,1024]{2,1,0:T(8,128)(2,1)}, u32[]{:S(2)}) copy-start(bf16[1,512,1024]{2,1,0:T(8,128)(2,1)} %param.11) | copy-start | bytes 3145732
  13.4 50.9 %all-to-all-start.1 = ((bf16[256,8,128]{0,2,1:T(8,128)(2,1)}), bf16[256,8,128]{0,2,1:T(8,128)(2,1)}, u32[]{:S(2)}, u32[]{:S(2)}) async-start(bf16[256,8,128]{0,2,1:T(8,128)(2,1)} %bitcast.157), calls=%async_computation.1 | async-start | bytes 1048576 | tf_op jit(solution)/shard_map/all_to_all | solution.py:82
  22.1 12.7 %copy-start.7 = (bf16[1,512,1024]{1,2,0:T(8,128)(2,1)S(1)}, bf16[1,512,1024]{1,2,0:T(8,128)(2,1)}, u32[]{:S(2)}) copy-start(bf16[1,512,1024]{1,2,0:T(8,128)(2,1)} %copy.114) | copy-start | bytes 3145732
  42.4 20.5 %copy-start.6 = (bf16[1,512,1024]{2,1,0:T(8,128)(2,1)S(1)}, bf16[1,512,1024]{2,1,0:T(8,128)(2,1)}, u32[]{:S(2)}) copy-start(bf16[1,512,1024]{2,1,0:T(8,128)(2,1)} %param.10) | copy-start | bytes 3145732
  52.4 16.8 %collective-permute-start = (bf16[256,128]{1,0:T(8,128)(2,1)}, bf16[256,128]{1,0:T(8,128)(2,1)}, u32[]{:S(2)}, u32[]{:S(2)}) collective-permute-start(bf16[256,128]{1,0:T(8,128)(2,1)} %bitcast.167), channel_id=1, source_target_pairs={{0,4},{4,0},{8,12},{12,8},{16,20},{20,16},{24,28},{28,24},{1,5},{5... | collective-permute-start | bytes 196616 | tf_op jit(solution)/shard_map/ppermute | solution.py:31
  56.0 18.0 %collective-permute-start.1 = (bf16[256,128]{1,0:T(8,128)(2,1)}, bf16[256,128]{1,0:T(8,128)(2,1)}, u32[]{:S(2)}, u32[]{:S(2)}) collective-permute-start(bf16[256,128]{1,0:T(8,128)(2,1)} %bitcast.166), channel_id=1, source_target_pairs={{0,8},{4,12},{8,0},{12,4},{16,24},{20,28},{24,16},{28,20},{1,9},{5... | collective-permute-start | bytes 196616 | tf_op jit(solution)/shard_map/ppermute | solution.py:31
  58.2 18.2 %collective-permute-start.2 = (bf16[256,128]{1,0:T(8,128)(2,1)}, bf16[256,128]{1,0:T(8,128)(2,1)}, u32[]{:S(2)}, u32[]{:S(2)}) collective-permute-start(bf16[256,128]{1,0:T(8,128)(2,1)} %bitcast.165), channel_id=1, source_target_pairs={{0,12},{4,8},{8,4},{12,0},{16,28},{20,24},{24,20},{28,16},{1,13},{... | collective-permute-start | bytes 196616 | tf_op jit(solution)/shard_map/ppermute | solution.py:31
  58.3 18.9 %collective-permute-start.3 = (bf16[256,128]{1,0:T(8,128)(2,1)S(1)}, bf16[256,128]{1,0:T(8,128)(2,1)}, u32[]{:S(2)}, u32[]{:S(2)}) collective-permute-start(bf16[256,128]{1,0:T(8,128)(2,1)S(1)} %bitcast.164), channel_id=1, source_target_pairs={{0,16},{4,20},{8,24},{12,28},{16,0},{20,4},{24,8},{28,12},{1,17},{... | collective-permute-start | bytes 196616 | tf_op jit(solution)/shard_map/ppermute | solution.py:31
  61.4 16.7 %collective-permute-start.4 = (bf16[256,128]{1,0:T(8,128)(2,1)S(1)}, bf16[256,128]{1,0:T(8,128)(2,1)S(1)}, u32[]{:S(2)}, u32[]{:S(2)}) collective-permute-start(bf16[256,128]{1,0:T(8,128)(2,1)S(1)} %bitcast.163), channel_id=1, source_target_pairs={{0,20},{4,16},{8,28},{12,24},{16,4},{20,0},{24,12},{28,8},{1,21},{... | collective-permute-start | bytes 196616 | tf_op jit(solution)/shard_map/ppermute | solution.py:31
  64.4 32.8 %all-to-all-start = ((bf16[512,8,128]{0,2,1:T(8,128)(2,1)}), bf16[512,8,128]{0,2,1:T(8,128)(2,1)}, u32[]{:S(2)}, u32[]{:S(2)}) async-start(bf16[512,8,128]{0,2,1:T(8,128)(2,1)} %bitcast.154), calls=%async_computation | async-start | bytes 2097152 | tf_op jit(solution)/shard_map/all_to_all | solution.py:81
  69.2 21.0 %collective-permute-start.5 = (bf16[256,128]{1,0:T(8,128)(2,1)S(1)}, bf16[256,128]{1,0:T(8,128)(2,1)S(1)}, u32[]{:S(2)}, u32[]{:S(2)}) collective-permute-start(bf16[256,128]{1,0:T(8,128)(2,1)S(1)} %bitcast.169), channel_id=1, source_target_pairs={{0,24},{4,28},{8,16},{12,20},{16,8},{20,12},{24,0},{28,4},{1,25},{... | collective-permute-start | bytes 196616 | tf_op jit(solution)/shard_map/ppermute | solution.py:31
  74.0 17.8 %collective-permute-start.6 = (bf16[256,128]{1,0:T(8,128)(2,1)S(1)}, bf16[256,128]{1,0:T(8,128)(2,1)S(1)}, u32[]{:S(2)}, u32[]{:S(2)}) collective-permute-start(bf16[256,128]{1,0:T(8,128)(2,1)S(1)} %bitcast.168), channel_id=1, source_target_pairs={{0,28},{4,24},{8,20},{12,16},{16,12},{20,8},{24,4},{28,0},{1,29},{... | collective-permute-start | bytes 196616 | tf_op jit(solution)/shard_map/ppermute | solution.py:31
  99.4 84.3 %copy-start.12 = (s32[1,4,1]{1,2,0:T(1,128)S(1)}, s32[1,4,1]{1,2,0:T(1,128)}, u32[]{:S(2)}) copy-start(s32[1,4,1]{1,2,0:T(1,128)} %param.15) | copy-start | bytes 52
  99.4 85.0 %copy-start.1 = (s32[1,4]{1,0:T(1,128)S(1)}, s32[1,4]{1,0:T(1,128)}, u32[]{:S(2)}) copy-start(s32[1,4]{1,0:T(1,128)} %param.16) | copy-start | bytes 52
  99.4 86.3 %copy-start.10 = (s32[1,4,128]{2,1,0:T(4,128)S(1)}, s32[1,4,128]{2,1,0:T(4,128)}, u32[]{:S(2)}) copy-start(s32[1,4,128]{2,1,0:T(4,128)} %param.17) | copy-start | bytes 6148
  103.1 5.7 %copy-start.2 = (f32[2,1024,2048]{2,1,0:T(8,128)}, f32[2,1024,2048]{2,1,0:T(8,128)S(1)}, u32[]{:S(2)}) copy-start(f32[2,1024,2048]{2,1,0:T(8,128)S(1)} %get-tuple-element.144) | copy-start | bytes 50331652 | tf_op jit(solution)/shard_map/while
  122.2 5.7 %copy-start.2 = (f32[2,1024,2048]{2,1,0:T(8,128)}, f32[2,1024,2048]{2,1,0:T(8,128)S(1)}, u32[]{:S(2)}) copy-start(f32[2,1024,2048]{2,1,0:T(8,128)S(1)} %get-tuple-element.144) | copy-start | bytes 50331652 | tf_op jit(solution)/shard_map/while
  141.3 5.7 %copy-start.2 = (f32[2,1024,2048]{2,1,0:T(8,128)}, f32[2,1024,2048]{2,1,0:T(8,128)S(1)}, u32[]{:S(2)}) copy-start(f32[2,1024,2048]{2,1,0:T(8,128)S(1)} %get-tuple-element.144) | copy-start | bytes 50331652 | tf_op jit(solution)/shard_map/while
  160.3 5.7 %copy-start.2 = (f32[2,1024,2048]{2,1,0:T(8,128)}, f32[2,1024,2048]{2,1,0:T(8,128)S(1)}, u32[]{:S(2)}) copy-start(f32[2,1024,2048]{2,1,0:T(8,128)S(1)} %get-tuple-element.144) | copy-start | bytes 50331652 | tf_op jit(solution)/shard_map/while
  175.8 40.9 %copy-start.11 = (f32[1024]{0:T(1024)S(1)}, f32[1024]{0:T(1024)}, u32[]{:S(2)}) copy-start(f32[1024]{0:T(1024)} %param.14) | copy-start | bytes 12292
  175.8 33.5 %all-to-all-start.2 = ((bf16[8,512,128]{2,1,0:T(8,128)(2,1)}), bf16[8,512,128]{2,1,0:T(8,128)(2,1)S(1)}, u32[]{:S(2)}, u32[]{:S(2)}) async-start(bf16[8,512,128]{2,1,0:T(8,128)(2,1)} %bitcast.159), calls=%async_computation.2 | async-start | bytes 2097152 | tf_op jit(solution)/shard_map/all_to_all | solution.py:87
  209.3 12.9 %all-to-all-start.3 = ((bf16[4,2,128]{2,1,0:T(2,128)(2,1)}), bf16[4,2,128]{2,1,0:T(2,128)(2,1)S(1)}, u32[]{:S(2)}, u32[]{:S(2)}) async-start(bf16[4,2,128]{2,1,0:T(2,128)(2,1)} %select_convert_fusion), calls=%async_computation.3 | async-start | bytes 4096 | tf_op jit(solution)/shard_map/all_to_all | solution.py:119
  222.2 30.2 %all-to-all-start.4 = ((bf16[4,2,128,1024]{3,2,1,0:T(8,128)(2,1)}), bf16[4,2,128,1024]{3,2,1,0:T(8,128)(2,1)}, u32[]{:S(2)}, u32[]{:S(2)}) async-start(bf16[4,2,128,1024]{3,2,1,0:T(8,128)(2,1)} %select_select_fusion), calls=%async_computation.4 | async-start | bytes 4194304 | tf_op jit(solution)/shard_map/all_to_all | solution.py:118
  (4 other events, 10.2 us)
